TPU v7x, 32 devices: a whole 2x2x4 slice. The times are simulated.
32 devices in a mesh: grp: 2 (over y), sec: 4 (over z), blk: 2 (over x), op: 2 (over core).
Axes of the slice: x: 2, y: 2, z: 4, core: 2. Of those that a mesh axis runs over, the one named last changes fastest.
Arguments:
- ground_state: bfloat16 [48, 512, 512], P(('grp', 'sec'), 'blk'), parts along dimension 0, may hold values from -6 to 6
- op_matrices: bfloat16 [16, 512, 512], P(('grp', 'op')), parts along dimension 0, may hold values from -0.25 to 0.25
- shift_map: int32 [16, 24], P('grp'), parts along dimension 0, may hold values from 0 to 23, as said below
- new_slot: int32 [48], P('grp'), parts along dimension 0, may hold values from 0 to 23, as said below
- env_ground: bfloat16 [48, 512, 512], P(('grp', 'sec'), 'blk'), parts along dimension 0, may hold values from -0.25 to 0.25
- env_src: int32 [48, 3], P('grp'), parts along dimension 0, may hold values from 0 to 23, as said below
- env_coef: float32 [48, 3], P('grp'), parts along dimension 0, may hold values from 0.3 to 1
Outputs:
- grown_env: bfloat16 [16, 24, 512, 512], P(('grp', 'op'), 'sec', 'blk'), parts along dimension 0
There are 2 independent parts, one for each index of `grp`. A program takes and returns all parts, laid end to end along the dimension named above; each array names one. Nothing has to cross between parts.
Inputs may be any that keep to these rules, and one draw needn't show every extreme that they name: Each row o maps the 24 ground sectors one to one onto the N+1 sectors. Within each group of 4 consecutive operators, among the pairs (o, s) with one value of s // 6, at most 7 have new_slot[shift_map[o, s]] // 6 equal to one value, and 7 is reached for every value of s // 6. A permutation: N+1 sector t is stored at slot new_slot[t]. For the N+1 sectors t with one value of new_slot[t] // 6, at most 6 of the entries env_src[t, k] have one value of env_src[t, k] // 6, and 6 is reached for every value of new_slot[t] // 6.
All inputs are finite; a program needn't handle non-finite values.
Results may differ from a plain program's by a relative error of at most 0.0057.
Values may be sent and summed in bfloat16 or wider, within the bound.
No kernel may reach another device: no remote copies, remote signals or barrier semaphores. Data moves between devices by JAX's collectives and lax.ppermute only.
A program may use at most 64 MiB of HBM per device.

v0:
```python
import jax
import jax.numpy as jnp
from jax import lax
from jax.sharding import PartitionSpec as P


def pair_ranks(pair_key):
    counter = jnp.arange(pair_key.shape[0])
    same_pair = pair_key[:, None] == pair_key[None, :]
    earlier = counter[None, :] < counter[:, None]
    return jnp.sum((same_pair & earlier).astype(jnp.int32), axis=1)


def local(ground_state, op_matrices, shift_map, new_slot, env_ground, env_src, env_coef):
    owner_count = lax.axis_size("sec")
    owner = lax.axis_index("sec")
    op_group = lax.axis_index("op")
    sec_dev, row_count, columns = ground_state.shape
    ops_dev = op_matrices.shape[0]
    env_terms = env_src.shape[1]
    sectors = sec_dev * owner_count
    capacity = (sec_dev * ops_dev + owner_count - 1) // owner_count + 1
    env_capacity = (sec_dev * env_terms + owner_count - 1) // owner_count + 1
    dest_all = jnp.take(new_slot, shift_map)
    dest_grp = lax.dynamic_slice_in_dim(dest_all, op_group * ops_dev, ops_dev, 0)
    source_of = jnp.argsort(dest_grp, axis=1)
    sources = lax.dynamic_slice_in_dim(source_of, owner * sec_dev, sec_dev, 1)
    products = jnp.einsum(
        "srd,ode->sore", ground_state, op_matrices, preferred_element_type=jnp.float32
    ).astype(jnp.bfloat16)
    entry_ids = jnp.arange(sectors * ops_dev)
    entry_sector = entry_ids // ops_dev
    entry_dest = dest_grp[entry_ids % ops_dev, entry_sector]
    ranking = pair_ranks(entry_sector // sec_dev * owner_count + entry_dest // sec_dev)
    positions = lax.dynamic_slice_in_dim(
        entry_dest // sec_dev * capacity + ranking, owner * sec_dev * ops_dev, sec_dev * ops_dev
    )
    outgoing = jnp.zeros((owner_count * capacity, row_count, columns), jnp.bfloat16)
    outgoing = outgoing.at[positions].set(products.reshape(sec_dev * ops_dev, row_count, columns))
    incoming = lax.all_to_all(outgoing, "sec", split_axis=0, concat_axis=0, tiled=True)
    wanted = sources * ops_dev + jnp.arange(ops_dev)[:, None]
    locate = sources // sec_dev * capacity + ranking[wanted]
    arrived = incoming[locate]
    sector_at = jnp.argsort(new_slot)
    my_sectors = lax.dynamic_slice_in_dim(sector_at, owner * sec_dev, sec_dev)
    my_coef = env_coef[my_sectors]
    flat_src = env_src[sector_at].reshape(-1)
    entry_slot = jnp.arange(sectors * env_terms) // env_terms
    ranking_env = pair_ranks(flat_src // sec_dev * owner_count + entry_slot // sec_dev)
    placing = entry_slot // sec_dev * env_capacity + ranking_env
    is_mine = flat_src // sec_dev == owner
    slot_ids = jnp.arange(owner_count * env_capacity)
    hit_table = ((placing[None, :] == slot_ids[:, None]) & is_mine[None, :]).astype(jnp.float32)
    local_table = ((flat_src - owner * sec_dev)[:, None] == jnp.arange(sec_dev)[None, :]).astype(
        jnp.float32
    )
    selector = jnp.dot(hit_table, local_table, precision=lax.Precision.HIGHEST).astype(jnp.bfloat16)
    outgoing_env = jnp.einsum(
        "pi,ird->prd", selector, env_ground, preferred_element_type=jnp.float32
    ).astype(jnp.bfloat16)
    incoming_env = lax.all_to_all(outgoing_env, "sec", split_axis=0, concat_axis=0, tiled=True)
    mine_entries = (owner * sec_dev + jnp.arange(sec_dev))[:, None] * env_terms + jnp.arange(
        env_terms
    )[None, :]
    locate_env = flat_src[mine_entries] // sec_dev * env_capacity + ranking_env[mine_entries]
    blocks = incoming_env[locate_env].astype(jnp.float32)
    mixed = jnp.sum(my_coef[:, :, None, None] * blocks, axis=1)
    env_rounded = mixed.astype(jnp.bfloat16)
    grown_env = jnp.einsum(
        "olrd,lde->olre",
        arrived,
        lax.all_gather(env_rounded, "blk", axis=1, tiled=True),
        preferred_element_type=jnp.float32,
    )
    return grown_env.astype(jnp.bfloat16)


def solution(mesh):
    return jax.shard_map(
        local,
        mesh=mesh,
        in_specs=(
            P(("grp", "sec"), "blk", None),
            P(("grp", "op"), None, None),
            P("grp", None),
            P("grp"),
            P(("grp", "sec"), "blk", None),
            P("grp", None),
            P("grp", None),
        ),
        out_specs=P(("grp", "op"), "sec", "blk", None),
        check_vma=False,
    )
```

profile of v0, /device:TPU:0, one launch (start us, length us, event | category | flops | bytes accessed | tf_op | source)
XLA Modules:
  0.0 368.2 jit_solution(6414172959295741181)
XLA Ops:
  6.6 0.8 compare_select_fusion.2
  7.5 1.9 gather_fusion.5
  9.5 0.7 and_select_fusion
  10.2 1.5 gather_fusion.6
  11.7 0.2 convert_reduce_fusion
  11.9 2.3 sort.34
  14.2 0.8 copy.39
  15.0 0.6 gather_fusion.1
  15.7 0.2 convert_reduce_fusion.1
  15.9 0.2 fusion.9
  16.2 3.3 convolution_convert_fusion
  19.5 4.9 %copy.41 = bf16[24,256,512]{2,1,0:T(8,128)(2,1)} copy(bf16[24,256,512]{2,0,1:T(8,128)(2,1)S(1)} %convolution_convert_fusion) | data formatting | bytes 12582912 | tf_op jit(solution)/shard_map/convert_element_type | solution.py:60
  24.3 6.3 %all-to-all-start = ((bf16[24,256,512]{2,1,0:T(8,128)(2,1)}), bf16[24,256,512]{2,1,0:T(8,128)(2,1)}, u32[]{:S(2)}, u32[]{:S(2)}) async-start(bf16[24,256,512]{2,1,0:T(8,128)(2,1)} %copy.41), calls=%async_computation | async-start | bytes 12582912 | tf_op jit(solution)/shard_map/all_to_all | solution.py:61
  30.7 6.8 %convert_bitcast_fusion.1 = bf16[6,4,256,512]{2,3,0,1:T(8,128)(2,1)} fusion(bf16[4,512,512]{2,1,0:T(8,128)(2,1)S(1)} %copy-done, bf16[6,256,512]{2,1,0:T(8,128)(2,1)} %param.7), kind=kOutput, calls=%fused_computation.15 | convolution fusion | flops 3224371200 | bytes 9961472 | tf_op jit(solution)/shard_map/srd,ode->sore/dot_general | solution.py:28
  37.5 8.7 %copy.44 = bf16[6,4,256,512]{3,2,1,0:T(8,128)(2,1)} copy(bf16[6,4,256,512]{2,3,0,1:T(8,128)(2,1)} %convert_bitcast_fusion.1) | data formatting | bytes 12582912 | tf_op jit(solution)/shard_map/convert_element_type | solution.py:30
  46.1 3.8 %broadcast_in_dim.22 = bf16[28,256,512]{2,1,0:T(8,128)(2,1)} broadcast(bf16[]{:T(256)} %constant.123.clone.1), dimensions={} | broadcast | bytes 7340034 | tf_op jit(solution)/shard_map/broadcast_in_dim | solution.py:38
  49.9 16.2 %scatter_fusion = bf16[28,256,512]{2,1,0:T(8,128)(2,1)} fusion(bf16[28,256,512]{2,1,0:T(8,128)(2,1)} %broadcast_in_dim.22, s32[24]{0:T(128)S(1)} %get-tuple-element.13, bf16[24,256,512]{2,1,0:T(8,128)(2,1)} %bitcast.30), kind=kCustom, calls=%fused_computation.9 | custom fusion | bytes 18874464 | tf_op jit(solution)/shard_map/scatter | solution.py:39
  66.1 103.3 %all-to-all-done = bf16[24,256,512]{2,1,0:T(8,128)(2,1)} async-done(((bf16[24,256,512]{2,1,0:T(8,128)(2,1)}), bf16[24,256,512]{2,1,0:T(8,128)(2,1)}, u32[]{:S(2)}, u32[]{:S(2)}) %all-to-all-start) | async-done | bytes 6291488 | tf_op jit(solution)/shard_map/all_to_all | solution.py:61
  169.4 5.4 %all-to-all-start.1 = ((bf16[28,256,512]{2,1,0:T(8,128)(2,1)}), bf16[28,256,512]{2,1,0:T(8,128)(2,1)}, u32[]{:S(2)}, u32[]{:S(2)}) async-start(bf16[28,256,512]{2,1,0:T(8,128)(2,1)} %scatter_fusion), calls=%async_computation.1 | async-start | bytes 14680064 | tf_op jit(solution)/shard_map/all_to_all | solution.py:40
  174.8 0.2 all-gather.2.cloned.1.call-start
  175.3 0.7 gather_fusion.3
  176.0 0.7 gather_fusion.2
  177.2 0.6 gather_fusion
  177.8 6.8 %gather_fusion.4 = bf16[18,256,512]{2,1,0:T(8,128)(2,1)} fusion(bf16[24,256,512]{2,1,0:T(8,128)(2,1)} %all-to-all-done, s32[1024]{0:T(1024)S(1)} %pad_clamp_fusion.3), kind=kCustom, calls=%fused_computation.4 | custom fusion | bytes 9437256 | tf_op jit(solution)/shard_map/gather | solution.py:66
  184.5 3.4 fusion
  187.9 1.6 copy.42
  189.6 0.8 sort.35
  190.6 0.7 gather_fusion.7
  191.7 143.5 %all-to-all-done.1 = bf16[28,256,512]{2,1,0:T(8,128)(2,1)} async-done(((bf16[28,256,512]{2,1,0:T(8,128)(2,1)}), bf16[28,256,512]{2,1,0:T(8,128)(2,1)}, u32[]{:S(2)}, u32[]{:S(2)}) %all-to-all-start.1) | async-done | bytes 7340064 | tf_op jit(solution)/shard_map/all_to_all | solution.py:40
  335.2 7.6 %gather_fusion.8 = bf16[24,256,512]{2,1,0:T(8,128)(2,1)} fusion(bf16[28,256,512]{2,1,0:T(8,128)(2,1)} %all-to-all-done.1, s32[1024]{0:T(1024)S(1)} %pad_clamp_fusion), kind=kCustom, calls=%fused_computation.8 | custom fusion | bytes 12583008 | tf_op jit(solution)/shard_map/gather | solution.py:43
  342.7 10.0 %convert_bitcast_fusion = bf16[4,6,256,512]{2,3,0,1:T(8,128)(2,1)} fusion(bf16[4,6,256,512]{3,2,1,0:T(8,128)(2,1)} %bitcast.32, bf16[6,512,512]{1,2,0:T(8,128)(2,1)} %all-gather.2.cloned.1.call-done), kind=kOutput, calls=%fused_computation.14 | convolution fusion | flops 3224371200 | bytes 15728640 | tf_op jit(solution)/shard_map/olrd,lde->olre/dot_general | solution.py:69
  352.7 8.6 %copy.50 = bf16[4,6,256,512]{3,2,1,0:T(8,128)(2,1)} copy(bf16[4,6,256,512]{2,3,0,1:T(8,128)(2,1)} %convert_bitcast_fusion) | data formatting | bytes 12582912 | tf_op jit(solution)/shard_map/convert_element_type | solution.py:75
  (50 shorter events, 1.9 us)
Async XLA Ops:
  6.5 24.1 %copy-start = (bf16[4,512,512]{2,1,0:T(8,128)(2,1)S(1)}, bf16[4,512,512]{2,1,0:T(8,128)(2,1)}, u32[]{:S(2)}) copy-start(bf16[4,512,512]{2,1,0:T(8,128)(2,1)} %param.8) | copy-start | bytes 6291460
  24.3 145.1 %all-to-all-start = ((bf16[24,256,512]{2,1,0:T(8,128)(2,1)}), bf16[24,256,512]{2,1,0:T(8,128)(2,1)}, u32[]{:S(2)}, u32[]{:S(2)}) async-start(bf16[24,256,512]{2,1,0:T(8,128)(2,1)} %copy.41), calls=%async_computation | async-start | bytes 12582912 | tf_op jit(solution)/shard_map/all_to_all | solution.py:61
  169.4 165.7 %all-to-all-start.1 = ((bf16[28,256,512]{2,1,0:T(8,128)(2,1)}), bf16[28,256,512]{2,1,0:T(8,128)(2,1)}, u32[]{:S(2)}, u32[]{:S(2)}) async-start(bf16[28,256,512]{2,1,0:T(8,128)(2,1)} %scatter_fusion), calls=%async_computation.1 | async-start | bytes 14680064 | tf_op jit(solution)/shard_map/all_to_all | solution.py:40
  174.8 2.2 copy-start.2
  174.8 167.9 %all-gather.2.cloned.1.call-start = ((), (), s32[]{:S(2)}) async-start(), calls=%async_computation.2 | async-start | bytes 4718592 | tf_op jit(solution)/shard_map/all_gather | solution.py:72
  342.7 18.7 %copy-start.1 = (bf16[4,512,512]{2,1,0:T(8,128)(2,1)S(1)}, bf16[4,512,512]{2,1,0:T(8,128)(2,1)}, u32[]{:S(2)}) copy-start(bf16[4,512,512]{2,1,0:T(8,128)(2,1)} %param.8) | copy-start | bytes 6291460
Sparse Core Ops, SparseCore 0:
  189.6 46.1 all-gather.1
where the time goes:
time: 369 us; the launch traced here: 368 us
  waiting for transfers between devices  247 us (67%)
  local copies, waits for them, and re-layouts  66.8 us (18%)
  matrix products  20.3 us (6%)
  between operations  13.5 us (4%)
  starting transfers between devices  12 us (3%)
  other arithmetic  8.77 us (2%)
    all_to_all x1, waiting for transfers between devices, local(): lax.all_to_all(outgoing, 'sec', split_axis=0, concat_axis=0, tiled=True)  143 us
    all_to_all x1, waiting for transfers between devices, local(): lax.all_to_all(outgoing_env, 'sec', split_axis=0, concat_axis=0, tiled=True)  103 us
    scatter x1, local copies, waits for them, and re-layouts, local(): outgoing.at[positions]  16.2 us
    dot_general x1, matrix products, local(): jnp.einsum('olrd,lde->olre', arrived, lax.all_gather(env_rounded, 'blk',...  10 us
    convert_element_type x1, local copies, waits for them, and re-layouts, local(): products = jnp.einsum('srd,ode->sore', ground_state, op_matrices, preferr...  8.66 us
    convert_element_type x1, local copies, waits for them, and re-layouts, local(): return grown_env.astype(jnp.bfloat16)  8.64 us
    gather x1, local copies, waits for them, and re-layouts, local(): arrived = incoming[locate]  7.57 us
  transfers between devices with their start and end apart: 3, of which 2 were waited for; matrix products, arithmetic and copies ran while one was open for 16% of the time, Pallas kernels for 0%

commit v1 on v0

--- a/solution.py
+++ b/solution.py
@@ -1,7 +1,39 @@
+import functools
 import jax
 import jax.numpy as jnp
 from jax import lax
 from jax.sharding import PartitionSpec as P
+from jax.lax import axis_index, axis_size, ppermute
+
+
+def attach_skins(s0, d0, buf):
+    res = s0.shape
+    passed = s0.reshape(*res[:d0], buf, res[d0] // buf, *res[d0 + 1 :])
+    return jnp.moveaxis(passed, d0, 0)
+
+
+def figure_enter(target, array_dim):
+    h_now = list(target.shape[1:])
+    h_now[array_dim] *= target.shape[0]
+    return jnp.moveaxis(target, 0, array_dim).reshape(h_now)
+
+
+def view_the_files(local_values, named_axis, field, body):
+    local_out, block_out = (axis_size(named_axis), axis_index(named_axis))
+    now = attach_skins(local_values, field, local_out)
+    queue = [now[block_out]]
+    i0 = 1
+    while i0 < local_out:
+        tmp = now[(block_out + i0) % local_out]
+        queue.append(
+            ppermute(tmp, named_axis, perm=[(rr, (rr + i0) % local_out) for rr in range(local_out)])
+        )
+        i0 += 1
+    now = jnp.stack(queue)[(block_out - jnp.arange(local_out)) % local_out]
+    return figure_enter(now, body)
+
+
+treat_points_all = functools.partial(view_the_files, named_axis="sec", field=0, body=0)
 
 
 def pair_ranks(pair_key):
@@ -58,7 +90,7 @@
     outgoing_env = jnp.einsum(
         "pi,ird->prd", selector, env_ground, preferred_element_type=jnp.float32
     ).astype(jnp.bfloat16)
-    incoming_env = lax.all_to_all(outgoing_env, "sec", split_axis=0, concat_axis=0, tiled=True)
+    incoming_env = treat_points_all(outgoing_env)
     mine_entries = (owner * sec_dev + jnp.arange(sec_dev))[:, None] * env_terms + jnp.arange(
         env_terms
     )[None, :]

time: 369 us -> 446 us (1.21)
  waiting for transfers between devices: 247 us -> 308 us
  local copies, waits for them, and re-layouts: 66.8 us -> 78.2 us
  other arithmetic: 8.77 us -> 14.6 us
    ppermute x0 -> x3, waiting for transfers between devices: none -> 275 us  [view_the_files(): ppermute(tmp, named_axis, perm=[(rr, (rr + i0) % local_out) for rr in ran...]
    all_to_all x1, waiting for transfers between devices: 143 us -> 0.01 us  [local(): lax.all_to_all(outgoing, 'sec', split_axis=0, concat_axis=0, tiled=True)]
    all_to_all x1 -> x0, waiting for transfers between devices: 103 us -> none  [local(): lax.all_to_all(outgoing_env, 'sec', split_axis=0, concat_axis=0, tiled=True)]
    all_gather x1, waiting for transfers between devices: 0.01 us -> 33.2 us  [local(): lax.all_gather(env_rounded, 'blk', axis=1, tiled=True)]
    all_to_all x1 -> x0, starting transfers between devices: 6.32 us -> none  [local(): lax.all_to_all(outgoing_env, 'sec', split_axis=0, concat_axis=0, tiled=True)]
    gather x0 -> x1, local copies, waits for them, and re-layouts: none -> 6.3 us  [view_the_files(): now = jnp.stack(queue)[(block_out - jnp.arange(local_out)) % local_out]]
    another operation x0 -> x1, other arithmetic: none -> 5.78 us  [view_the_files(): now = jnp.stack(queue)[(block_out - jnp.arange(local_out)) % local_out]]
    ppermute x0 -> x3, starting transfers between devices: none -> 5.17 us  [view_the_files(): ppermute(tmp, named_axis, perm=[(rr, (rr + i0) % local_out) for rr in ran...]
  transfers between devices with their start and end apart: 3 -> 5, of which waited for: 2 -> 3; matrix products, arithmetic and copies ran while one was open for 16% -> 11% of each run, Pallas kernels for 0% -> 0%
where the time goes in v1:
time: 446 us; the launch traced here: 445 us
  waiting for transfers between devices  308 us (69%)
  local copies, waits for them, and re-layouts  78.2 us (18%)
  matrix products  19.2 us (4%)
  other arithmetic  14.6 us (3%)
  between operations  13.5 us (3%)
  starting transfers between devices  11.7 us (3%)
    ppermute x3, waiting for transfers between devices, view_the_files(): ppermute(tmp, named_axis, perm=[(rr, (rr + i0) % local_out) for rr in ran...  275 us
    all_gather x1, waiting for transfers between devices, local(): lax.all_gather(env_rounded, 'blk', axis=1, tiled=True)  33.2 us
    scatter x1, local copies, waits for them, and re-layouts, local(): outgoing.at[positions]  16.2 us
    dot_general x1, matrix products, local(): jnp.einsum('olrd,lde->olre', arrived, lax.all_gather(env_rounded, 'blk',...  10 us
  transfers between devices with their start and end apart: 5, of which 3 were waited for; matrix products, arithmetic and copies ran while one was open for 11% of the time, Pallas kernels for 0%

profile of v1, /device:TPU:0, one launch (start us, length us, event | category | flops | bytes accessed | tf_op | source)
XLA Modules:
  0.0 445.1 jit_solution(14796988350252759221)
XLA Ops:
  6.6 0.8 compare_select_fusion.2
  7.5 1.9 gather_fusion.6
  9.5 0.7 and_select_fusion
  10.2 1.5 gather_fusion.7
  11.9 2.3 sort.34
  14.2 6.8 %convert_bitcast_fusion.1 = bf16[6,4,256,512]{2,3,0,1:T(8,128)(2,1)} fusion(bf16[4,512,512]{2,1,0:T(8,128)(2,1)S(1)} %copy-done, bf16[6,256,512]{2,1,0:T(8,128)(2,1)} %param.7), kind=kOutput, calls=%fused_computation.17 | convolution fusion | flops 3224371200 | bytes 9961472 | tf_op jit(solution)/shard_map/srd,ode->sore/dot_general | solution.py:60
  21.0 8.7 %copy.44 = bf16[6,4,256,512]{3,2,1,0:T(8,128)(2,1)} copy(bf16[6,4,256,512]{2,3,0,1:T(8,128)(2,1)} %convert_bitcast_fusion.1) | data formatting | bytes 12582912 | tf_op jit(solution)/shard_map/convert_element_type | solution.py:62
  29.7 3.8 broadcast_in_dim.22
  33.6 16.2 %scatter_fusion = bf16[28,256,512]{2,1,0:T(8,128)(2,1)} fusion(bf16[28,256,512]{2,1,0:T(8,128)(2,1)} %broadcast_in_dim.22, s32[24]{0:T(128)S(1)} %get-tuple-element.17, bf16[24,256,512]{2,1,0:T(8,128)(2,1)} %bitcast.44), kind=kCustom, calls=%fused_computation.10 | custom fusion | bytes 18874464 | tf_op jit(solution)/shard_map/scatter | solution.py:71
  49.8 6.5 %all-to-all-start = ((bf16[28,256,512]{2,1,0:T(8,128)(2,1)}), bf16[28,256,512]{2,1,0:T(8,128)(2,1)}, u32[]{:S(2)}, u32[]{:S(2)}) async-start(bf16[28,256,512]{2,1,0:T(8,128)(2,1)} %scatter_fusion), calls=%async_computation | async-start | bytes 14680064 | tf_op jit(solution)/shard_map/all_to_all | solution.py:72
  56.4 0.6 gather_fusion.1
  57.5 2.1 convolution_convert_fusion
  59.7 5.0 %copy.41 = bf16[24,256,512]{2,1,0:T(8,128)(2,1)} copy(bf16[24,256,512]{2,0,1:T(8,128)(2,1)S(1)} %convolution_convert_fusion) | data formatting | bytes 12582912 | tf_op jit(solution)/shard_map/convert_element_type | solution.py:92
  64.6 5.2 %constant_dynamic-slice_fusion.1 = (bf16[1,6,256,512]{3,2,1,0:T(8,128)(2,1)S(1)}, bf16[6,256,512]{2,1,0:T(8,128)(2,1)}, bf16[6,256,512]{2,1,0:T(8,128)(2,1)}, bf16[6,256,512]{2,1,0:T(8,128)(2,1)}) fusion(bf16[4,6,256,512]{3,2,1,0:T(8,128)(2,1)} %bitcast.43, s32[]{:T(128)S(6)} %select_n.255, s32[]{:T(128)S(6)} %select_n.261, s32[]{:T(128)S(6)} %select_n.259, ...), kind=kLoop, calls=%fused_computation.82 | loop fusion | bytes 12582928 | tf_op jit(solution)/shard_map/dynamic_slice | solution.py:24
  69.8 4.3 collective-permute-start.2
  74.1 0.9 collective-permute-start
  75.1 0.7 gather_fusion.4
  75.8 0.7 gather_fusion.3
  77.1 0.6 gather_fusion
  77.7 131.7 %collective-permute-done.2 = bf16[6,256,512]{2,1,0:T(8,128)(2,1)} collective-permute-done((bf16[6,256,512]{2,1,0:T(8,128)(2,1)}, bf16[6,256,512]{2,1,0:T(8,128)(2,1)}, u32[]{:S(2)}, u32[]{:S(2)}) %collective-permute-start.2) | collective-permute-done | bytes 1572896 | tf_op jit(solution)/shard_map/ppermute | solution.py:29
  209.4 143.1 %collective-permute-done.1 = bf16[6,256,512]{2,1,0:T(8,128)(2,1)} collective-permute-done((bf16[6,256,512]{2,1,0:T(8,128)(2,1)}, bf16[6,256,512]{2,1,0:T(8,128)(2,1)}, u32[]{:S(2)}, u32[]{:S(2)}) %collective-permute-start.1) | collective-permute-done | bytes 1572896 | tf_op jit(solution)/shard_map/ppermute | solution.py:29
  352.5 5.8 %pad_maximum_fusion = bf16[4,6,256,512]{3,2,1,0:T(8,128)(2,1)} fusion(bf16[1,6,256,512]{3,2,1,0:T(8,128)(2,1)} %bitcast.7, bf16[1,6,256,512]{3,2,1,0:T(8,128)(2,1)} %bitcast.5, bf16[1,6,256,512]{3,2,1,0:T(8,128)(2,1)} %bitcast.3, bf16[1,6,256,512]{3,2,1,0:T(8,128)(2,1)S(1)} %get-tuple-element.13), kind=kLoop, calls=%fused_computation.13 | loop fusion | flops 9437184 | bytes 12582912 | tf_op jit(solution)/shard_map/stack | solution.py:32
  358.3 6.3 %gather_fusion.2 = bf16[4,6,256,512]{3,2,1,0:T(8,128)(2,1)} fusion(bf16[4,6,256,512]{3,2,1,0:T(8,128)(2,1)} %pad_maximum_fusion, s32[1024]{0:T(1024)S(1)} %pad_clamp_fusion.5), kind=kCustom, calls=%fused_computation.2 | custom fusion | bytes 12582928 | tf_op jit(solution)/shard_map/gather | solution.py:32
  364.6 6.8 %gather_fusion.5 = bf16[18,256,512]{2,1,0:T(8,128)(2,1)} fusion(bf16[24,256,512]{2,1,0:T(8,128)(2,1)} %bitcast.45, s32[1024]{0:T(1024)S(1)} %pad_clamp_fusion.3), kind=kCustom, calls=%fused_computation.5 | custom fusion | bytes 9437256 | tf_op jit(solution)/shard_map/gather | solution.py:98
  371.3 3.4 fusion
  374.7 1.6 copy.42
  376.4 0.8 sort.35
  377.4 0.7 gather_fusion.8
  378.5 8.0 %gather_fusion.9 = bf16[24,256,512]{2,1,0:T(8,128)(2,1)} fusion(bf16[28,256,512]{2,1,0:T(8,128)(2,1)} %all-to-all-done, s32[1024]{0:T(1024)S(1)} %pad_clamp_fusion), kind=kCustom, calls=%fused_computation.9 | custom fusion | bytes 12583008 | tf_op jit(solution)/shard_map/gather | solution.py:75
  386.5 33.2 %all-gather.2.cloned.1.call-done = bf16[6,512,512]{1,2,0:T(8,128)(2,1)} async-done(((bf16[6,256,512]{1,2,0:T(8,128)(2,1)}), bf16[6,512,512]{1,2,0:T(8,128)(2,1)}) %all-gather.2.cloned.1.call-update) | async-done | bytes 3145744 | tf_op jit(solution)/shard_map/all_gather | solution.py:104
  419.6 10.0 %convert_bitcast_fusion = bf16[4,6,256,512]{2,3,0,1:T(8,128)(2,1)} fusion(bf16[4,6,256,512]{3,2,1,0:T(8,128)(2,1)} %bitcast.47, bf16[6,512,512]{1,2,0:T(8,128)(2,1)} %all-gather.2.cloned.1.call-done), kind=kOutput, calls=%fused_computation.16 | convolution fusion | flops 3224371200 | bytes 15728640 | tf_op jit(solution)/shard_map/olrd,lde->olre/dot_general | solution.py:101
  429.6 8.6 %copy.50 = bf16[4,6,256,512]{3,2,1,0:T(8,128)(2,1)} copy(bf16[4,6,256,512]{2,3,0,1:T(8,128)(2,1)} %convert_bitcast_fusion) | data formatting | bytes 12582912 | tf_op jit(solution)/shard_map/convert_element_type | solution.py:107
  (63 shorter events, 2.6 us)
Async XLA Ops:
  6.5 7.6 %copy-start = (bf16[4,512,512]{2,1,0:T(8,128)(2,1)S(1)}, bf16[4,512,512]{2,1,0:T(8,128)(2,1)}, u32[]{:S(2)}) copy-start(bf16[4,512,512]{2,1,0:T(8,128)(2,1)} %param.8) | copy-start | bytes 6291460
  49.8 6.5 %copy-start.3 = (s32[24,3]{0,1:T(4,128)S(1)}, s32[24,3]{0,1:T(4,128)}, u32[]{:S(2)}) copy-start(s32[24,3]{0,1:T(4,128)} %param.12) | copy-start | bytes 868
  49.8 7.8 %copy-start.2 = (bf16[6,256,512]{2,1,0:T(8,128)(2,1)S(1)}, bf16[6,256,512]{2,1,0:T(8,128)(2,1)}, u32[]{:S(2)}) copy-start(bf16[6,256,512]{2,1,0:T(8,128)(2,1)} %param.11) | copy-start | bytes 4718596
  49.8 328.7 %all-to-all-start = ((bf16[28,256,512]{2,1,0:T(8,128)(2,1)}), bf16[28,256,512]{2,1,0:T(8,128)(2,1)}, u32[]{:S(2)}, u32[]{:S(2)}) async-start(bf16[28,256,512]{2,1,0:T(8,128)(2,1)} %scatter_fusion), calls=%async_computation | async-start | bytes 14680064 | tf_op jit(solution)/shard_map/all_to_all | solution.py:72
  56.3 363.4 %all-gather.2.cloned.1.call-start = ((), (), s32[]{:S(2)}) async-start(), calls=%async_computation.1 | async-start | bytes 4718592 | tf_op jit(solution)/shard_map/all_gather | solution.py:104
  69.8 7.1 %copy-start.4 = (f32[24,3]{0,1:T(4,128)S(1)}, f32[24,3]{0,1:T(4,128)}, u32[]{:S(2)}) copy-start(f32[24,3]{0,1:T(4,128)} %param.13) | copy-start | bytes 868
  69.8 139.6 %collective-permute-start.2 = (bf16[6,256,512]{2,1,0:T(8,128)(2,1)}, bf16[6,256,512]{2,1,0:T(8,128)(2,1)}, u32[]{:S(2)}, u32[]{:S(2)}) collective-permute-start(bf16[6,256,512]{2,1,0:T(8,128)(2,1)} %get-tuple-element.14), channel_id=1, source_target_pairs={{0,12},{4,0},{8,4},{12,8},{1,13},{5,1},{9,5},{13,9},{2,14},{6,2},{... | collective-permute-start | bytes 4718600 | tf_op jit(solution)/shard_map/ppermute | solution.py:29
  74.1 278.4 %collective-permute-start.1 = (bf16[6,256,512]{2,1,0:T(8,128)(2,1)}, bf16[6,256,512]{2,1,0:T(8,128)(2,1)}, u32[]{:S(2)}, u32[]{:S(2)}) collective-permute-start(bf16[6,256,512]{2,1,0:T(8,128)(2,1)} %get-tuple-element.15), channel_id=1, source_target_pairs={{0,8},{4,12},{8,0},{12,4},{1,9},{5,13},{9,1},{13,5},{2,10},{6,14},... | collective-permute-start | bytes 4718600 | tf_op jit(solution)/shard_map/ppermute | solution.py:29
  74.1 278.4 %collective-permute-start = (bf16[6,256,512]{2,1,0:T(8,128)(2,1)}, bf16[6,256,512]{2,1,0:T(8,128)(2,1)}, u32[]{:S(2)}, u32[]{:S(2)}) collective-permute-start(bf16[6,256,512]{2,1,0:T(8,128)(2,1)} %get-tuple-element.16), channel_id=1, source_target_pairs={{0,4},{4,8},{8,12},{12,0},{1,5},{5,9},{9,13},{13,1},{2,6},{6,10},{... | collective-permute-start | bytes 4718600 | tf_op jit(solution)/shard_map/ppermute | solution.py:29
  419.6 18.6 %copy-start.1 = (bf16[4,512,512]{2,1,0:T(8,128)(2,1)S(1)}, bf16[4,512,512]{2,1,0:T(8,128)(2,1)}, u32[]{:S(2)}) copy-start(bf16[4,512,512]{2,1,0:T(8,128)(2,1)} %param.8) | copy-start | bytes 6291460
Sparse Core Ops, SparseCore 0:
  376.4 43.1 all-gather.1
